TPU v7x, 256 devices: a whole 4x4x8 slice. The times are simulated.
256 devices in a mesh: group: 8 (over z), row: 32 (over y, x, core).
Axes of the slice: x: 4, y: 4, z: 8, core: 2. Of those that a mesh axis runs over, the one named last changes fastest.
Arguments:
- start_basis: float32 [2048, 16, 128], P(('group', 'row')), may hold values from -6 to 6
- tiles: bfloat16 [2048, 16, 128, 128], P(('group', 'row')), may hold values from -60000 to 60000
- tile_cols: int32 [2048, 16], P(('group', 'row')), may hold values from 0 to 75, as said below
- tile_count: int32 [2048], P(('group', 'row')), may hold values from 10 to 16, as said below
- recv_list: int32 [8, 32, 32, 2], P('group', 'row'), may hold values from -1 to 2047, as said below
Outputs:
- krylov: float32 [3, 2048, 16, 128], P(None, ('group', 'row'))
Inputs may be any that keep to these rules, and one draw needn't show every extreme that they name: For each reader device and each other device of its range, recv_list names distinct blocks of that peer in its first slots and -1 in the rest; a reader's own entry is all -1; every reader gets exactly 2 blocks from some peer. tile_cols never names an empty receive slot, nor a rim slot of a range that does not exist (before the first or after the last group); every filled receive slot and every existing rim slot is named by some tile slot below 10. `tile_count`: every device has a row block with all 16 tiles live.
All inputs are finite; a program needn't handle non-finite values.
Results may differ from a plain program's by a relative error of at most 0.0003.
Values sent between devices are 32-bit elements; how exact they have to be, the bound alone decides.
A program may use at most 64 MiB of HBM per device.

v0:
```python
import jax
import jax.numpy as jnp
from jax import lax
from jax.sharding import PartitionSpec as P

SLOTS = 2
RIM = 2
ITERS = 3


def padded(x, sides, width):
    for axis, dim in sides:
        count, length = (lax.axis_size(axis), x.shape[dim])
        up = [(i, (i + 1) % count) for i in range(count - 1)]
        down = [(j, i) for i, j in up]
        last = lax.slice_in_dim(x, length - width, length, axis=dim)
        leading = lax.slice_in_dim(x, 0, width, axis=dim)
        before = lax.ppermute(last, axis, up)
        after = lax.ppermute(leading, axis, down)
        x = jnp.concatenate([before, x, after], axis=dim)
    return x


def orthonormal(applied, gram_sum, row_total):
    vectors = applied.shape[1]
    factor = jnp.linalg.cholesky(gram_sum / row_total)
    inverse = lax.linalg.triangular_solve(
        factor, jnp.eye(vectors, dtype=jnp.float32), left_side=True, lower=True
    )
    return jnp.einsum("kl,bli->bki", inverse, applied, precision=lax.Precision.HIGHEST)


def local(start_basis, tiles, tile_cols, tile_count, recv_list):
    groups = lax.axis_size("group")
    peers = lax.axis_size("row")
    group_at = lax.axis_index("group")
    blocks = tiles.shape[0]
    per_row = tiles.shape[1]
    tile_side = tiles.shape[2]
    row_total = groups * peers * blocks * tile_side
    live_mask = (jnp.arange(per_row, dtype=jnp.int32)[None, :] < tile_count[:, None]).astype(
        jnp.float32
    )
    wide_tiles = tiles.astype(jnp.float32)
    sum_sq = jnp.einsum(
        "btij,bt->bi", wide_tiles * wide_tiles, live_mask, precision=lax.Precision.HIGHEST
    )
    inv_root = (1e-06 + sum_sq) ** (-0.25)
    wanted = recv_list.reshape(peers, SLOTS)
    gather_pick = jnp.clip(wanted - group_at * peers * blocks, 0, peers * blocks - 1).reshape(-1)
    results = []
    basis = start_basis
    for step_at in range(ITERS):
        scaled = basis * inv_root[:, None, :]
        rimmed = padded(scaled, (("group", 0),), RIM)
        group_all = lax.all_gather(scaled, "row", axis=0, tiled=True)
        received = jnp.take(group_all, gather_pick, axis=0)
        extended = jnp.concatenate([scaled, received, rimmed[:RIM], rimmed[blocks + RIM :]], axis=0)
        picked = jnp.take(extended, tile_cols, axis=0) * live_mask[:, :, None, None]
        product = jnp.einsum(
            "btij,btkj->bki",
            tiles,
            picked,
            precision=lax.Precision.HIGHEST,
            preferred_element_type=jnp.float32,
        )
        applied = product * inv_root[:, None, :]
        partial_value = jnp.einsum("bki,bli->kl", applied, applied, precision=lax.Precision.HIGHEST)
        gram_sum = lax.psum(partial_value, ("group", "row"))
        basis = orthonormal(applied, gram_sum, row_total)
        results.append(basis)
    return jnp.stack(results)


def solution(mesh):
    placed = (
        P(("group", "row"), None, None),
        P(("group", "row"), None, None, None),
        P(("group", "row"), None),
        P(("group", "row")),
        P("group", "row", None, None),
    )
    return jax.shard_map(
        local,
        mesh=mesh,
        in_specs=placed,
        out_specs=P(None, ("group", "row"), None, None),
        check_vma=False,
    )
```

profile of v0, /device:TPU:1, one launch (start us, length us, event | category | flops | bytes accessed | tf_op | source)
XLA Modules:
  0.0 434.7 jit_solution(10057653734697218750)
XLA Ops:
  6.6 4.5 %multiply_reduce_fusion = f32[8,16,128]{2,1,0:T(8,128)S(1)} fusion(bf16[8,16,128,128]{3,2,1,0:T(8,128)(2,1)} %param.13), kind=kLoop, calls=%fused_computation.6 | loop fusion | flops 6275072 | bytes 4259840 | tf_op jit(solution)/shard_map/btij,bt->bi/reduce_sum | solution.py:45
  12.8 4.4 %collective-permute-start = (f32[2,16,128]{2,1,0:T(8,128)S(1)}, f32[2,16,128]{2,1,0:T(8,128)S(1)}, u32[]{:S(2)}, u32[]{:S(2)}) collective-permute-start(f32[2,16,128]{2,1,0:T(8,128)S(1)} %get-tuple-element.13), channel_id=1, source_target_pairs={{0,32},{32,64},{64,96},{96,128},{128,160},{160,192},{192,224},{1,3... | collective-permute-start | bytes 49160 | tf_op jit(solution)/shard_map/ppermute | solution.py:18
  17.2 1.3 collective-permute-start.1
  18.8 46.4 %all-gather.4.cloned.1.call-done = f32[256,16,128]{2,1,0:T(8,128)} async-done(((f32[8,16,128]{2,1,0:T(8,128)}), f32[256,16,128]{2,1,0:T(8,128)}) %all-gather.4.cloned.1.call-update) | async-done | bytes 2097168 | tf_op jit(solution)/shard_map/all_gather | solution.py:56
  65.2 2.2 gather_fusion
  69.2 5.2 %fusion.2 = f32[8,16,128]{2,1,0:T(8,128)S(1)} fusion(bf16[8,16,128,128]{3,2,1,0:T(8,128)(2,1)} %param.13, f32[8,16,16,128]{3,2,1,0:T(8,128)S(1)} %bitcast.92, f32[8,16]{1,0:T(8,128)S(1)} %get-tuple-element.15, pred[8,16]{1,0:T(8,128)(4,1)S(1)} %get-tuple-element.21, f32[8,128]{1,0:T(8,128)S(1)} %add_power_fusion), kind=kOutput, calls=%fused_computation.13 | convolution fusion | flops 403193856 | bytes 5313152 | tf_op jit(solution)/shard_map/btij,btkj->bki/dot_general | solution.py:60
  74.6 75.6 %psum.21 = f32[16,16]{0,1:T(8,128)S(1)} all-reduce(f32[16,16]{0,1:T(8,128)S(1)} %convolution_bitcast_fusion.9), channel_id=1, replica_groups=mesh['group'=8,'row'=32] {'group','row'}, use_global_device_ids=true, to_apply=%region_1.0 | all-reduce | flops 256 | bytes 2048 | tf_op jit(solution)/shard_map/psum | solution.py:69
  150.3 1.5 cholesky.59
  153.0 1.2 custom-call.7
  156.1 2.9 collective-permute-start.2
  159.1 1.3 collective-permute-start.3
  160.4 41.2 %all-gather.6.cloned.1.call-done = f32[256,16,128]{2,1,0:T(8,128)} async-done(((f32[8,16,128]{2,1,0:T(8,128)}), f32[256,16,128]{2,1,0:T(8,128)}) %all-gather.6.cloned.1.call-update) | async-done | bytes 2097168 | tf_op jit(solution)/shard_map/all_gather | solution.py:56
  201.6 2.2 gather_fusion.2
  205.6 5.2 %fusion.1 = f32[8,16,128]{2,1,0:T(8,128)S(1)} fusion(bf16[8,16,128,128]{3,2,1,0:T(8,128)(2,1)} %param.13, f32[8,16,16,128]{3,2,1,0:T(8,128)S(1)} %bitcast.93, f32[8,16]{1,0:T(8,128)S(1)} %get-tuple-element.15, pred[8,16]{1,0:T(8,128)(4,1)S(1)} %get-tuple-element.21, f32[8,128]{1,0:T(8,128)S(1)} %add_power_fusion), kind=kOutput, calls=%fused_computation.11 | convolution fusion | flops 403193856 | bytes 5313152 | tf_op jit(solution)/shard_map/btij,btkj->bki/dot_general | solution.py:60
  211.0 75.6 %psum.22 = f32[16,16]{0,1:T(8,128)S(1)} all-reduce(f32[16,16]{0,1:T(8,128)S(1)} %convolution_bitcast_fusion.7), channel_id=1, replica_groups=mesh['group'=8,'row'=32] {'group','row'}, use_global_device_ids=true, to_apply=%region_4.9 | all-reduce | flops 256 | bytes 2048 | tf_op jit(solution)/shard_map/psum | solution.py:69
  286.6 1.5 cholesky.70
  289.4 1.2 custom-call.8
  292.5 2.9 collective-permute-start.4
  295.4 1.3 collective-permute-start.5
  296.7 41.3 %all-gather.8.cloned.1.call-done = f32[256,16,128]{2,1,0:T(8,128)} async-done(((f32[8,16,128]{2,1,0:T(8,128)}), f32[256,16,128]{2,1,0:T(8,128)}) %all-gather.8.cloned.1.call-update) | async-done | bytes 2097168 | tf_op jit(solution)/shard_map/all_gather | solution.py:56
  338.0 2.2 gather_fusion.4
  342.0 5.2 %fusion = f32[8,16,128]{2,1,0:T(8,128)S(1)} fusion(bf16[8,16,128,128]{3,2,1,0:T(8,128)(2,1)} %param.13, f32[8,16,16,128]{3,2,1,0:T(8,128)S(1)} %bitcast.91, f32[8,16]{1,0:T(8,128)S(1)} %get-tuple-element.15, pred[8,16]{1,0:T(8,128)(4,1)S(1)} %get-tuple-element.21, f32[8,128]{1,0:T(8,128)S(1)} %add_power_fusion), kind=kOutput, calls=%fused_computation.9 | convolution fusion | flops 403193856 | bytes 5313152 | tf_op jit(solution)/shard_map/btij,btkj->bki/dot_general | solution.py:60
  347.4 75.6 %psum.23 = f32[16,16]{0,1:T(8,128)S(1)} all-reduce(f32[16,16]{0,1:T(8,128)S(1)} %convolution_bitcast_fusion.5), channel_id=1, replica_groups=mesh['group'=8,'row'=32] {'group','row'}, use_global_device_ids=true, to_apply=%region_5.10 | all-reduce | flops 256 | bytes 2048 | tf_op jit(solution)/shard_map/psum | solution.py:69
  423.0 1.5 cholesky.81
  (74 shorter events, 18.1 us)
Async XLA Ops:
  6.5 4.5 %copy-start.1 = (s32[8,16]{1,0:T(8,128)S(1)}, s32[8,16]{1,0:T(8,128)}, u32[]{:S(2)}) copy-start(s32[8,16]{1,0:T(8,128)} %param.14) | copy-start | bytes 1540
  6.5 4.5 %copy-start.3 = (s32[8]{0:T(128)S(1)}, s32[8]{0:T(128)}, u32[]{:S(2)}) copy-start(s32[8]{0:T(128)} %param.15) | copy-start | bytes 100
  6.5 4.8 %copy-start = (f32[8,16,128]{2,1,0:T(8,128)S(1)}, f32[8,16,128]{2,1,0:T(8,128)}, u32[]{:S(2)}) copy-start(f32[8,16,128]{2,1,0:T(8,128)} %param.12) | copy-start | bytes 196612
  6.5 12.0 %copy-start.2 = (s32[1,1,32,2]{2,3,1,0:T(2,128)S(1)}, s32[1,1,32,2]{2,3,1,0:T(2,128)}, u32[]{:S(2)}) copy-start(s32[1,1,32,2]{2,3,1,0:T(2,128)} %param.16) | copy-start | bytes 772
  6.5 58.7 %all-gather.4.cloned.1.call-start = ((), (), s32[]{:S(2)}) async-start(), calls=%async_computation | async-start | bytes 2162688 | tf_op jit(solution)/shard_map/all_gather | solution.py:56
  12.0 189.6 %all-gather.6.cloned.1.call-start = ((), (), s32[]{:S(2)}) async-start(), calls=%async_computation.1 | async-start | bytes 2162688 | tf_op jit(solution)/shard_map/all_gather | solution.py:56
  12.8 54.8 %collective-permute-start = (f32[2,16,128]{2,1,0:T(8,128)S(1)}, f32[2,16,128]{2,1,0:T(8,128)S(1)}, u32[]{:S(2)}, u32[]{:S(2)}) collective-permute-start(f32[2,16,128]{2,1,0:T(8,128)S(1)} %get-tuple-element.13), channel_id=1, source_target_pairs={{0,32},{32,64},{64,96},{96,128},{128,160},{160,192},{192,224},{1,3... | collective-permute-start | bytes 49160 | tf_op jit(solution)/shard_map/ppermute | solution.py:18
  17.2 50.4 %collective-permute-start.1 = (f32[2,16,128]{2,1,0:T(8,128)S(1)}, f32[2,16,128]{2,1,0:T(8,128)S(1)}, u32[]{:S(2)}, u32[]{:S(2)}) collective-permute-start(f32[2,16,128]{2,1,0:T(8,128)S(1)} %get-tuple-element.14), channel_id=1, source_target_pairs={{32,0},{64,32},{96,64},{128,96},{160,128},{192,160},{224,192},{33,... | collective-permute-start | bytes 49160 | tf_op jit(solution)/shard_map/ppermute | solution.py:19
  155.3 182.7 %all-gather.8.cloned.1.call-start = ((), (), s32[]{:S(2)}) async-start(), calls=%async_computation.2 | async-start | bytes 2162688 | tf_op jit(solution)/shard_map/all_gather | solution.py:56
  156.1 47.8 %collective-permute-start.2 = (f32[2,16,128]{2,1,0:T(8,128)S(1)}, f32[2,16,128]{2,1,0:T(8,128)S(1)}, u32[]{:S(2)}, u32[]{:S(2)}) collective-permute-start(f32[2,16,128]{2,1,0:T(8,128)S(1)} %get-tuple-element.10), channel_id=1, source_target_pairs={{0,32},{32,64},{64,96},{96,128},{128,160},{160,192},{192,224},{1,3... | collective-permute-start | bytes 49160 | tf_op jit(solution)/shard_map/ppermute | solution.py:18
  159.1 44.9 %collective-permute-start.3 = (f32[2,16,128]{2,1,0:T(8,128)S(1)}, f32[2,16,128]{2,1,0:T(8,128)S(1)}, u32[]{:S(2)}, u32[]{:S(2)}) collective-permute-start(f32[2,16,128]{2,1,0:T(8,128)S(1)} %get-tuple-element.12), channel_id=1, source_target_pairs={{32,0},{64,32},{96,64},{128,96},{160,128},{192,160},{224,192},{33,... | collective-permute-start | bytes 49160 | tf_op jit(solution)/shard_map/ppermute | solution.py:19
  292.5 47.9 %collective-permute-start.4 = (f32[2,16,128]{2,1,0:T(8,128)S(1)}, f32[2,16,128]{2,1,0:T(8,128)S(1)}, u32[]{:S(2)}, u32[]{:S(2)}) collective-permute-start(f32[2,16,128]{2,1,0:T(8,128)S(1)} %get-tuple-element.6), channel_id=1, source_target_pairs={{0,32},{32,64},{64,96},{96,128},{128,160},{160,192},{192,224},{1,3... | collective-permute-start | bytes 49160 | tf_op jit(solution)/shard_map/ppermute | solution.py:18
  295.4 44.9 %collective-permute-start.5 = (f32[2,16,128]{2,1,0:T(8,128)S(1)}, f32[2,16,128]{2,1,0:T(8,128)S(1)}, u32[]{:S(2)}, u32[]{:S(2)}) collective-permute-start(f32[2,16,128]{2,1,0:T(8,128)S(1)} %get-tuple-element.8), channel_id=1, source_target_pairs={{32,0},{64,32},{96,64},{128,96},{160,128},{192,160},{224,192},{33,... | collective-permute-start | bytes 49160 | tf_op jit(solution)/shard_map/ppermute | solution.py:19
Sparse Core Ops, SparseCore 0:
  12.1 53.0 all-gather.3
  155.5 46.1 all-gather.5
  291.8 46.1 all-gather.7
where the time goes:
time: 436 us; the launch traced here: 435 us
  blocking collectives  227 us (52%)
  waiting for transfers between devices  129 us (30%)
  other arithmetic  21 us (5%)
  matrix products  18.7 us (4%)
  starting transfers between devices  14.2 us (3%)
  between operations  13.4 us (3%)
  local copies, waits for them, and re-layouts  11.6 us (3%)
    psum x3, blocking collectives, local(): gram_sum = lax.psum(partial_value, ('group', 'row'))  227 us
    all_gather x3, waiting for transfers between devices, local(): group_all = lax.all_gather(scaled, 'row', axis=0, tiled=True)  129 us
    dot_general x3, matrix products, local(): jnp.einsum('btij,btkj->bki', tiles, picked, precision=lax.Precision.HIGHE...  15.5 us
    ppermute x3, starting transfers between devices, padded(): before = lax.ppermute(last, axis, up)  10.2 us
  transfers between devices with their start and end apart: 9, of which 3 were waited for; matrix products, arithmetic and copies ran while one was open for 2% of the time, Pallas kernels for 0%

commit v1 on v0

--- a/solution.py
+++ b/solution.py
@@ -2,6 +2,7 @@
 import jax.numpy as jnp
 from jax import lax
 from jax.sharding import PartitionSpec as P
+from jax.lax import all_gather
 
 SLOTS = 2
 RIM = 2
@@ -66,7 +67,7 @@
         )
         applied = product * inv_root[:, None, :]
         partial_value = jnp.einsum("bki,bli->kl", applied, applied, precision=lax.Precision.HIGHEST)
-        gram_sum = lax.psum(partial_value, ("group", "row"))
+        gram_sum = jnp.sum(all_gather(partial_value, ("group", "row")), axis=0)
         basis = orthonormal(applied, gram_sum, row_total)
         results.append(basis)
     return jnp.stack(results)

time: 436 us -> 416 us (0.954)
  blocking collectives: 227 us -> 207 us
    psum x3 -> x0, blocking collectives: 227 us -> none  [local(): gram_sum = lax.psum(partial_value, ('group', 'row'))]
    all_gather x0 -> x3, blocking collectives: none -> 207 us  [local(): gram_sum = jnp.sum(all_gather(partial_value, ('group', 'row')), axis=0)]
where the time goes in v1:
time: 416 us; the launch traced here: 415 us
  blocking collectives  207 us (50%)
  waiting for transfers between devices  129 us (31%)
  other arithmetic  21.9 us (5%)
  matrix products  18.7 us (4%)
  starting transfers between devices  13.4 us (3%)
  between operations  13.4 us (3%)
  local copies, waits for them, and re-layouts  11.8 us (3%)
    all_gather x3, blocking collectives, local(): gram_sum = jnp.sum(all_gather(partial_value, ('group', 'row')), axis=0)  207 us
    all_gather x3, waiting for transfers between devices, local(): group_all = lax.all_gather(scaled, 'row', axis=0, tiled=True)  129 us
    dot_general x3, matrix products, local(): jnp.einsum('btij,btkj->bki', tiles, picked, precision=lax.Precision.HIGHE...  15.5 us
    ppermute x3, starting transfers between devices, padded(): before = lax.ppermute(last, axis, up)  9.46 us
  transfers between devices with their start and end apart: 9, of which 3 were waited for; matrix products, arithmetic and copies ran while one was open for 2% of the time, Pallas kernels for 0%

profile of v1, /device:TPU:1, one launch (start us, length us, event | category | flops | bytes accessed | tf_op | source)
XLA Modules:
  0.0 414.7 jit_solution(14175272219558175602)
XLA Ops:
  6.6 4.5 %multiply_reduce_fusion = f32[8,16,128]{2,1,0:T(8,128)S(1)} fusion(bf16[8,16,128,128]{3,2,1,0:T(8,128)(2,1)} %param.13), kind=kLoop, calls=%fused_computation.6 | loop fusion | flops 6275072 | bytes 4259840 | tf_op jit(solution)/shard_map/btij,bt->bi/reduce_sum | solution.py:46
  12.8 4.4 %collective-permute-start = (f32[2,16,128]{2,1,0:T(8,128)S(1)}, f32[2,16,128]{2,1,0:T(8,128)S(1)}, u32[]{:S(2)}, u32[]{:S(2)}) collective-permute-start(f32[2,16,128]{2,1,0:T(8,128)S(1)} %get-tuple-element.13), channel_id=1, source_target_pairs={{0,32},{32,64},{64,96},{96,128},{128,160},{160,192},{192,224},{1,3... | collective-permute-start | bytes 49160 | tf_op jit(solution)/shard_map/ppermute | solution.py:19
  17.2 1.3 collective-permute-start.1
  18.8 46.4 %all-gather.7.cloned.1.call-done = f32[256,16,128]{2,1,0:T(8,128)} async-done(((f32[8,16,128]{2,1,0:T(8,128)}), f32[256,16,128]{2,1,0:T(8,128)}) %all-gather.7.cloned.1.call-update) | async-done | bytes 2097168 | tf_op jit(solution)/shard_map/all_gather | solution.py:57
  65.2 2.2 gather_fusion
  69.2 5.2 %fusion.2 = f32[8,16,128]{2,1,0:T(8,128)S(1)} fusion(bf16[8,16,128,128]{3,2,1,0:T(8,128)(2,1)} %param.13, f32[8,16,16,128]{3,2,1,0:T(8,128)S(1)} %bitcast.98, f32[8,16]{1,0:T(8,128)S(1)} %get-tuple-element.15, pred[8,16]{1,0:T(8,128)(4,1)S(1)} %get-tuple-element.21, f32[8,128]{1,0:T(8,128)S(1)} %add_power_fusion), kind=kOutput, calls=%fused_computation.13 | convolution fusion | flops 403193856 | bytes 5313152 | tf_op jit(solution)/shard_map/btij,btkj->bki/dot_general | solution.py:61
  74.6 68.8 %all-gather = f32[4096,16]{1,0:T(8,128)S(1)} all-gather(f32[16,16]{1,0:T(8,128)S(1)} %convolution_bitcast_fusion.9), channel_id=2, replica_groups=mesh['group'=8,'row'=32] {'group','row'}, dimensions={0}, use_global_device_ids=true | all-gather | bytes 263168 | tf_op jit(solution)/shard_map/all_gather | solution.py:70
  143.9 1.5 cholesky.59
  146.7 1.2 custom-call.7
  149.7 2.5 collective-permute-start.2
  152.3 1.3 collective-permute-start.3
  153.6 41.1 %all-gather.9.cloned.1.call-done = f32[256,16,128]{2,1,0:T(8,128)} async-done(((f32[8,16,128]{2,1,0:T(8,128)}), f32[256,16,128]{2,1,0:T(8,128)}) %all-gather.9.cloned.1.call-update) | async-done | bytes 2097168 | tf_op jit(solution)/shard_map/all_gather | solution.py:57
  194.7 2.2 gather_fusion.2
  198.8 5.2 %fusion.1 = f32[8,16,128]{2,1,0:T(8,128)S(1)} fusion(bf16[8,16,128,128]{3,2,1,0:T(8,128)(2,1)} %param.13, f32[8,16,16,128]{3,2,1,0:T(8,128)S(1)} %bitcast.99, f32[8,16]{1,0:T(8,128)S(1)} %get-tuple-element.15, pred[8,16]{1,0:T(8,128)(4,1)S(1)} %get-tuple-element.21, f32[8,128]{1,0:T(8,128)S(1)} %add_power_fusion), kind=kOutput, calls=%fused_computation.11 | convolution fusion | flops 403193856 | bytes 5313152 | tf_op jit(solution)/shard_map/btij,btkj->bki/dot_general | solution.py:61
  204.1 69.0 %all-gather.1 = f32[4096,16]{1,0:T(8,128)S(1)} all-gather(f32[16,16]{1,0:T(8,128)S(1)} %convolution_bitcast_fusion.7), channel_id=3, replica_groups=mesh['group'=8,'row'=32] {'group','row'}, dimensions={0}, use_global_device_ids=true | all-gather | bytes 263168 | tf_op jit(solution)/shard_map/all_gather | solution.py:70
  273.6 1.5 cholesky.70
  276.3 1.2 custom-call.8
  279.4 2.5 collective-permute-start.4
  281.9 1.3 collective-permute-start.5
  283.2 41.2 %all-gather.11.cloned.1.call-done = f32[256,16,128]{2,1,0:T(8,128)} async-done(((f32[8,16,128]{2,1,0:T(8,128)}), f32[256,16,128]{2,1,0:T(8,128)}) %all-gather.11.cloned.1.call-update) | async-done | bytes 2097168 | tf_op jit(solution)/shard_map/all_gather | solution.py:57
  324.4 2.2 gather_fusion.4
  328.4 5.2 %fusion = f32[8,16,128]{2,1,0:T(8,128)S(1)} fusion(bf16[8,16,128,128]{3,2,1,0:T(8,128)(2,1)} %param.13, f32[8,16,16,128]{3,2,1,0:T(8,128)S(1)} %bitcast.97, f32[8,16]{1,0:T(8,128)S(1)} %get-tuple-element.15, pred[8,16]{1,0:T(8,128)(4,1)S(1)} %get-tuple-element.21, f32[8,128]{1,0:T(8,128)S(1)} %add_power_fusion), kind=kOutput, calls=%fused_computation.9 | convolution fusion | flops 403193856 | bytes 5313152 | tf_op jit(solution)/shard_map/btij,btkj->bki/dot_general | solution.py:61
  333.8 68.8 %all-gather.2 = f32[4096,16]{1,0:T(8,128)S(1)} all-gather(f32[16,16]{1,0:T(8,128)S(1)} %convolution_bitcast_fusion.5), channel_id=4, replica_groups=mesh['group'=8,'row'=32] {'group','row'}, dimensions={0}, use_global_device_ids=true | all-gather | bytes 263168 | tf_op jit(solution)/shard_map/all_gather | solution.py:70
  403.1 1.5 cholesky.81
  (80 shorter events, 19.2 us)
Async XLA Ops:
  6.5 4.5 %copy-start.1 = (s32[8,16]{1,0:T(8,128)S(1)}, s32[8,16]{1,0:T(8,128)}, u32[]{:S(2)}) copy-start(s32[8,16]{1,0:T(8,128)} %param.14) | copy-start | bytes 1540
  6.5 4.5 %copy-start.3 = (s32[8]{0:T(128)S(1)}, s32[8]{0:T(128)}, u32[]{:S(2)}) copy-start(s32[8]{0:T(128)} %param.15) | copy-start | bytes 100
  6.5 4.8 %copy-start = (f32[8,16,128]{2,1,0:T(8,128)S(1)}, f32[8,16,128]{2,1,0:T(8,128)}, u32[]{:S(2)}) copy-start(f32[8,16,128]{2,1,0:T(8,128)} %param.12) | copy-start | bytes 196612
  6.5 12.0 %copy-start.2 = (s32[1,1,32,2]{2,3,1,0:T(2,128)S(1)}, s32[1,1,32,2]{2,3,1,0:T(2,128)}, u32[]{:S(2)}) copy-start(s32[1,1,32,2]{2,3,1,0:T(2,128)} %param.16) | copy-start | bytes 772
  6.5 58.7 %all-gather.7.cloned.1.call-start = ((), (), s32[]{:S(2)}) async-start(), calls=%async_computation | async-start | bytes 2162688 | tf_op jit(solution)/shard_map/all_gather | solution.py:57
  12.0 182.8 %all-gather.9.cloned.1.call-start = ((), (), s32[]{:S(2)}) async-start(), calls=%async_computation.1 | async-start | bytes 2162688 | tf_op jit(solution)/shard_map/all_gather | solution.py:57
  12.8 54.8 %collective-permute-start = (f32[2,16,128]{2,1,0:T(8,128)S(1)}, f32[2,16,128]{2,1,0:T(8,128)S(1)}, u32[]{:S(2)}, u32[]{:S(2)}) collective-permute-start(f32[2,16,128]{2,1,0:T(8,128)S(1)} %get-tuple-element.13), channel_id=1, source_target_pairs={{0,32},{32,64},{64,96},{96,128},{128,160},{160,192},{192,224},{1,3... | collective-permute-start | bytes 49160 | tf_op jit(solution)/shard_map/ppermute | solution.py:19
  17.2 50.4 %collective-permute-start.1 = (f32[2,16,128]{2,1,0:T(8,128)S(1)}, f32[2,16,128]{2,1,0:T(8,128)S(1)}, u32[]{:S(2)}, u32[]{:S(2)}) collective-permute-start(f32[2,16,128]{2,1,0:T(8,128)S(1)} %get-tuple-element.14), channel_id=1, source_target_pairs={{32,0},{64,32},{96,64},{128,96},{160,128},{192,160},{224,192},{33,... | collective-permute-start | bytes 49160 | tf_op jit(solution)/shard_map/ppermute | solution.py:20
  149.0 175.5 %all-gather.11.cloned.1.call-start = ((), (), s32[]{:S(2)}) async-start(), calls=%async_computation.2 | async-start | bytes 2162688 | tf_op jit(solution)/shard_map/all_gather | solution.py:57
  149.7 47.3 %collective-permute-start.2 = (f32[2,16,128]{2,1,0:T(8,128)S(1)}, f32[2,16,128]{2,1,0:T(8,128)S(1)}, u32[]{:S(2)}, u32[]{:S(2)}) collective-permute-start(f32[2,16,128]{2,1,0:T(8,128)S(1)} %get-tuple-element.10), channel_id=1, source_target_pairs={{0,32},{32,64},{64,96},{96,128},{128,160},{160,192},{192,224},{1,3... | collective-permute-start | bytes 49160 | tf_op jit(solution)/shard_map/ppermute | solution.py:19
  152.3 44.8 %collective-permute-start.3 = (f32[2,16,128]{2,1,0:T(8,128)S(1)}, f32[2,16,128]{2,1,0:T(8,128)S(1)}, u32[]{:S(2)}, u32[]{:S(2)}) collective-permute-start(f32[2,16,128]{2,1,0:T(8,128)S(1)} %get-tuple-element.12), channel_id=1, source_target_pairs={{32,0},{64,32},{96,64},{128,96},{160,128},{192,160},{224,192},{33,... | collective-permute-start | bytes 49160 | tf_op jit(solution)/shard_map/ppermute | solution.py:20
  279.4 47.4 %collective-permute-start.4 = (f32[2,16,128]{2,1,0:T(8,128)S(1)}, f32[2,16,128]{2,1,0:T(8,128)S(1)}, u32[]{:S(2)}, u32[]{:S(2)}) collective-permute-start(f32[2,16,128]{2,1,0:T(8,128)S(1)} %get-tuple-element.6), channel_id=1, source_target_pairs={{0,32},{32,64},{64,96},{96,128},{128,160},{160,192},{192,224},{1,3... | collective-permute-start | bytes 49160 | tf_op jit(solution)/shard_map/ppermute | solution.py:19
  281.9 44.8 %collective-permute-start.5 = (f32[2,16,128]{2,1,0:T(8,128)S(1)}, f32[2,16,128]{2,1,0:T(8,128)S(1)}, u32[]{:S(2)}, u32[]{:S(2)}) collective-permute-start(f32[2,16,128]{2,1,0:T(8,128)S(1)} %get-tuple-element.8), channel_id=1, source_target_pairs={{32,0},{64,32},{96,64},{128,96},{160,128},{192,160},{224,192},{33,... | collective-permute-start | bytes 49160 | tf_op jit(solution)/shard_map/ppermute | solution.py:20
Sparse Core Ops, SparseCore 0:
  12.1 53.0 all-gather.6
  149.1 45.6 all-gather.8
  278.8 45.6 all-gather.10
